TPU v7x, 32 devices: a whole 2x2x4 slice. The times are simulated.
32 devices in a mesh: tm: 8 (over y, x, core), rows: 4 (over z).
Axes of the slice: x: 2, y: 2, z: 4, core: 2. Of those that a mesh axis runs over, the one named last changes fastest.
Arguments:
- frames_in: bfloat16 [32, 32, 32, 512], P('tm', 'rows'), may hold values from -6 to 6
- weight_in: bfloat16 [2, 512, 4608], P(None, 'rows'), may hold values from -0.09375 to 0.09375
- weight_out: bfloat16 [9, 2, 512, 512], P(None, None, 'rows'), may hold values from -0.015625 to 0.015625
- log_decay: float32 [512], replicated, may hold values from 0.0003125 to 0.06
- rotation: float32 [512], replicated, may hold values from -3.140625 to 3.140625
- start_state: float32 [32, 32, 2, 512], P('rows'), may hold values from -12 to 12
- skip_gain: float32 [512], replicated, may hold values from -1 to 1
Outputs:
- frames_out: bfloat16 [32, 32, 32, 512], P('tm', 'rows')
All inputs are finite; a program needn't handle non-finite values.
Results may differ from a plain program's by a relative error of at most 0.0047.
Values may be sent and summed in bfloat16 or wider, within the bound.
A program may use at most 128 MiB of HBM per device.

v0:
```python
import jax
import jax.numpy as jnp
from jax import lax
from jax.sharding import PartitionSpec as P


def passed_along(value, axis, steps):
    count = lax.axis_size(axis)
    first, last = (max(0, -steps), min(count, count - steps))
    return lax.ppermute(value, axis, [(source, source + steps) for source in range(first, last)])


def extended_2(cells, sides, width):
    for axis, dim in sides:
        count = lax.axis_size(axis)
        ends = count - 1
        head = lax.slice_in_dim(cells, 0, width, axis=dim)
        tail = lax.slice_in_dim(cells, cells.shape[dim] - width, cells.shape[dim], axis=dim)
        cells = jnp.concatenate(
            [
                lax.ppermute(tail, axis, [(i, (i + 1) % count) for i in range(ends)]),
                cells,
                lax.ppermute(head, axis, [((i + 1) % count, i) for i in range(ends)]),
            ],
            axis=dim,
        )
    return cells


def pad_field(field, rows_pad):
    widths = [(0, 0)] * field.ndim
    widths[1] = (rows_pad, rows_pad)
    widths[2] = (1, 1)
    return jnp.pad(field, widths)


def in_term(padded, piece, height, columns):
    parts, state_width, span = piece.shape
    channels = span // 9
    matrix = piece.reshape(parts * state_width, span)
    summed = jnp.zeros((padded.shape[0], height, columns, parts * state_width), jnp.float32)
    for tap_index in range(9):
        row_shift = tap_index // 3
        col_shift = tap_index % 3
        window = padded[:, row_shift : row_shift + height, col_shift : col_shift + columns, :]
        weight_tap = matrix[:, tap_index * channels : (tap_index + 1) * channels]
        summed = summed + lax.dot_general(
            window, weight_tap, (((3,), (1,)), ((), ())), preferred_element_type=jnp.float32
        )
    return summed.reshape(padded.shape[0], height, columns, parts, state_width)


def out_term(padded_held, piece, height, columns):
    summed = jnp.zeros((padded_held.shape[0], height, columns, piece.shape[3]), jnp.float32)
    for tap_index in range(9):
        row_shift = tap_index // 3
        col_shift = tap_index % 3
        window = padded_held[:, row_shift : row_shift + height, col_shift : col_shift + columns]
        summed = summed + lax.dot_general(
            window,
            piece[tap_index],
            (((3, 4), (0, 1)), ((), ())),
            preferred_element_type=jnp.float32,
        )
    return summed


def run_states(driven, start_re, start_im, log_rate, angle):
    frame_count = driven.shape[0]
    modulus = jnp.exp(-log_rate)
    lam_re = modulus * jnp.cos(angle)
    lam_im = modulus * jnp.sin(angle)
    is_first = lax.axis_index("tm") == 0
    begin_re = jnp.where(is_first, start_re, jnp.float32(0.0))
    begin_im = jnp.where(is_first, start_im, jnp.float32(0.0))

    def advance(carried, forcing):
        state_re, state_im = carried
        force_re, force_im = forcing
        new_re = lam_re * state_re - lam_im * state_im + force_re
        new_im = lam_re * state_im + lam_im * state_re + force_im
        return ((new_re, new_im), (new_re, new_im))

    (tail_re, tail_im), (local_re, local_im) = lax.scan(
        advance, (begin_re, begin_im), (driven[..., 0, :], driven[..., 1, :])
    )
    span_mod = jnp.exp(-log_rate * frame_count)
    span_re = span_mod * jnp.cos(angle * frame_count)
    span_im = span_mod * jnp.sin(angle * frame_count)

    def relay(turn_index, carried):
        prior_re, prior_im = carried
        sent_re = span_re * prior_re - span_im * prior_im + tail_re
        sent_im = span_re * prior_im + span_im * prior_re + tail_im
        return passed_along((sent_re, sent_im), "tm", 1)

    carry_re, carry_im = lax.fori_loop(
        0, lax.axis_size("tm") - 1, relay, (jnp.zeros_like(tail_re), jnp.zeros_like(tail_im))
    )
    step_count = jnp.arange(1, frame_count + 1, dtype=jnp.float32)[:, None, None, None]
    power_mod = jnp.exp(-log_rate * step_count)
    power_re = power_mod * jnp.cos(angle * step_count)
    power_im = power_mod * jnp.sin(angle * step_count)
    states_re = local_re + power_re * carry_re - power_im * carry_im
    states_im = local_im + power_re * carry_im + power_im * carry_re
    return jnp.stack([states_re, states_im], 3).astype(jnp.bfloat16)


def on_device(frames_in, weight_in, weight_out, log_decay, rotation, start_state, skip_gain):
    frame_count, band_rows, columns, channels = frames_in.shape
    extended = extended_2(frames_in, (("rows", 1),), 1)
    padded = pad_field(extended, 0)
    driven = in_term(
        padded, lax.all_gather(weight_in, "rows", axis=1, tiled=True), band_rows, columns
    )
    held = run_states(driven, start_state[:, :, 0, :], start_state[:, :, 1, :], log_decay, rotation)
    held = extended_2(held, (("rows", 1),), 1)
    held_padded = pad_field(held, 0)
    mixing = out_term(
        held_padded, lax.all_gather(weight_out, "rows", axis=2, tiled=True), band_rows, columns
    )
    pre_act = mixing + skip_gain * frames_in.astype(jnp.float32)
    return jax.nn.gelu(pre_act, approximate=False).astype(jnp.bfloat16)


def solution(mesh):
    return jax.shard_map(
        on_device,
        mesh=mesh,
        in_specs=(
            P("tm", "rows", None, None),
            P(None, "rows", None),
            P(None, None, "rows", None),
            P(),
            P(),
            P("rows", None, None, None),
            P(),
        ),
        out_specs=P("tm", "rows", None, None),
        check_vma=False,
    )
```

profile of v0, /device:TPU:12, one launch (start us, length us, event | category | flops | bytes accessed | tf_op | source)
XLA Modules:
  0.0 405.1 jit_solution(16774444298382258066)
XLA Ops:
  9.0 3.5 collective-permute-start.2
  20.2 153.8 %all-gather.3.cloned.1.call-done = bf16[2,512,4608]{2,1,0:T(8,128)(2,1)} async-done(((bf16[2,128,4608]{2,1,0:T(8,128)(2,1)}), bf16[2,512,4608]{2,1,0:T(8,128)(2,1)}) %all-gather.3.cloned.1.call-update) | async-done | bytes 9437200 | tf_op jit(solution)/shard_map/all_gather | solution.py:114
  200.0 11.9 %add_add_fusion.1 = f32[4,8,32,1024]{3,2,1,0:T(8,128)} fusion(f32[4,8,32,1024]{3,2,1,0:T(8,128)S(1)} %fusion.55, f32[4,8,32,1024]{3,2,1,0:T(8,128)} %fusion.63, f32[4,8,32,1024]{3,2,1,0:T(8,128)} %fusion.65, f32[4,8,32,1024]{3,2,1,0:T(8,128)} %fusion.67, f32[4,8,32,1024]{3,2,1,0:T(8,128)} %fusion.68, f32[4,8,32,1024]{3,2,1,0:T(8,128)} %fusion.70, ...), kind=kOutput, calls=%fused_computation.11 | convolution fusion | flops 1082130432 | bytes 39845888 | tf_op jit(solution)/shard_map/dot_general | solution.py:47
  211.9 6.6 %reshape.132 = f32[4,8,32,2,512]{4,3,2,1,0:T(2,128)} reshape(f32[4,8,32,1024]{3,2,1,0:T(8,128)} %add_add_fusion.1) | data formatting | bytes 8388608 | tf_op jit(solution)/shard_map/reshape | solution.py:50
  218.5 7.9 %fusion.83 = (f32[4,8,32,1,512]{4,3,2,1,0:T(1,128)S(1)}, f32[4,8,32,1,512]{4,3,2,1,0:T(1,128)S(1)}) fusion(f32[4,8,32,2,512]{4,3,2,1,0:T(2,128)} %reshape.132), kind=kLoop, calls=%fused_computation.146 | loop fusion | bytes 8388608 | tf_op jit(solution)/shard_map/slice | solution.py:85
  231.6 9.8 %while.28 = (s32[]{:T(128)}, f32[8,32,512]{2,1,0:T(8,128)S(1)}, f32[8,32,512]{2,1,0:T(8,128)S(1)}, f32[4,8,32,512]{3,2,1,0:T(8,128)}, f32[4,8,32,512]{3,2,1,0:T(...) while((s32[]{:T(128)}, f32[8,32,512]{2,1,0:T(8,128)S(1)}, ...), condition=%wide.region_1.2_spmd, body=%wide.region_0.1_spmd.sunk | while | flops 1048578 | bytes 4199013 | solution.py:84
  241.5 120.9 %while.29 = (s32[]{:T(128)}, f32[8,32,512]{2,1,0:T(8,128)S(1)}, f32[8,32,512]{2,1,0:T(8,128)S(1)}, f32[512]{0:T(512)S(1)}, f32[512]{0:T(512)S(1)}, /*index=5*/f3...) while((s32[]{:T(128)}, f32[8,32,512]{2,1,0:T(8,128)S(1)}, f32[8,32,512]{2,1,0:T(8,128)S(1)}, ...), condition=%wide.region_3.4_spmd, body=%wide.region_2.3_spmd.sunk | while | flops 1048578 | bytes 7344293 | solution.py:97
  247.2 6.0 %collective-permute-done = f32[8,32,512]{2,1,0:T(8,128)S(1)} collective-permute-done((f32[8,32,512]{2,1,0:T(8,128)S(1)}, f32[8,32,512]{2,1,0:T(8,128)S(1)}, u32[]{:S(2)}, u32[]{:S(2)}) %collective-permute-start) | collective-permute-done | bytes 524320 | tf_op jit(solution)/shard_map/while/body/eval_jaxpr/ppermute | solution.py:10
  253.2 5.6 %collective-permute-done.1 = f32[8,32,512]{2,1,0:T(8,128)S(1)} collective-permute-done((f32[8,32,512]{2,1,0:T(8,128)S(1)}, f32[8,32,512]{2,1,0:T(8,128)S(1)}, u32[]{:S(2)}, u32[]{:S(2)}) %collective-permute-start.1) | collective-permute-done | bytes 524320 | tf_op jit(solution)/shard_map/while/body/eval_jaxpr/ppermute | solution.py:10
  263.6 6.9 %collective-permute-done = f32[8,32,512]{2,1,0:T(8,128)S(1)} collective-permute-done((f32[8,32,512]{2,1,0:T(8,128)S(1)}, f32[8,32,512]{2,1,0:T(8,128)S(1)}, u32[]{:S(2)}, u32[]{:S(2)}) %collective-permute-start) | collective-permute-done | bytes 524320 | tf_op jit(solution)/shard_map/while/body/eval_jaxpr/ppermute | solution.py:10
  270.4 5.6 %collective-permute-done.1 = f32[8,32,512]{2,1,0:T(8,128)S(1)} collective-permute-done((f32[8,32,512]{2,1,0:T(8,128)S(1)}, f32[8,32,512]{2,1,0:T(8,128)S(1)}, u32[]{:S(2)}, u32[]{:S(2)}) %collective-permute-start.1) | collective-permute-done | bytes 524320 | tf_op jit(solution)/shard_map/while/body/eval_jaxpr/ppermute | solution.py:10
  280.2 7.5 %collective-permute-done = f32[8,32,512]{2,1,0:T(8,128)S(1)} collective-permute-done((f32[8,32,512]{2,1,0:T(8,128)S(1)}, f32[8,32,512]{2,1,0:T(8,128)S(1)}, u32[]{:S(2)}, u32[]{:S(2)}) %collective-permute-start) | collective-permute-done | bytes 524320 | tf_op jit(solution)/shard_map/while/body/eval_jaxpr/ppermute | solution.py:10
  287.7 5.6 %collective-permute-done.1 = f32[8,32,512]{2,1,0:T(8,128)S(1)} collective-permute-done((f32[8,32,512]{2,1,0:T(8,128)S(1)}, f32[8,32,512]{2,1,0:T(8,128)S(1)}, u32[]{:S(2)}, u32[]{:S(2)}) %collective-permute-start.1) | collective-permute-done | bytes 524320 | tf_op jit(solution)/shard_map/while/body/eval_jaxpr/ppermute | solution.py:10
  297.4 7.5 %collective-permute-done = f32[8,32,512]{2,1,0:T(8,128)S(1)} collective-permute-done((f32[8,32,512]{2,1,0:T(8,128)S(1)}, f32[8,32,512]{2,1,0:T(8,128)S(1)}, u32[]{:S(2)}, u32[]{:S(2)}) %collective-permute-start) | collective-permute-done | bytes 524320 | tf_op jit(solution)/shard_map/while/body/eval_jaxpr/ppermute | solution.py:10
  305.0 5.6 %collective-permute-done.1 = f32[8,32,512]{2,1,0:T(8,128)S(1)} collective-permute-done((f32[8,32,512]{2,1,0:T(8,128)S(1)}, f32[8,32,512]{2,1,0:T(8,128)S(1)}, u32[]{:S(2)}, u32[]{:S(2)}) %collective-permute-start.1) | collective-permute-done | bytes 524320 | tf_op jit(solution)/shard_map/while/body/eval_jaxpr/ppermute | solution.py:10
  314.7 7.5 %collective-permute-done = f32[8,32,512]{2,1,0:T(8,128)S(1)} collective-permute-done((f32[8,32,512]{2,1,0:T(8,128)S(1)}, f32[8,32,512]{2,1,0:T(8,128)S(1)}, u32[]{:S(2)}, u32[]{:S(2)}) %collective-permute-start) | collective-permute-done | bytes 524320 | tf_op jit(solution)/shard_map/while/body/eval_jaxpr/ppermute | solution.py:10
  322.3 5.6 %collective-permute-done.1 = f32[8,32,512]{2,1,0:T(8,128)S(1)} collective-permute-done((f32[8,32,512]{2,1,0:T(8,128)S(1)}, f32[8,32,512]{2,1,0:T(8,128)S(1)}, u32[]{:S(2)}, u32[]{:S(2)}) %collective-permute-start.1) | collective-permute-done | bytes 524320 | tf_op jit(solution)/shard_map/while/body/eval_jaxpr/ppermute | solution.py:10
  332.0 7.5 %collective-permute-done = f32[8,32,512]{2,1,0:T(8,128)S(1)} collective-permute-done((f32[8,32,512]{2,1,0:T(8,128)S(1)}, f32[8,32,512]{2,1,0:T(8,128)S(1)}, u32[]{:S(2)}, u32[]{:S(2)}) %collective-permute-start) | collective-permute-done | bytes 524320 | tf_op jit(solution)/shard_map/while/body/eval_jaxpr/ppermute | solution.py:10
  339.5 5.6 %collective-permute-done.1 = f32[8,32,512]{2,1,0:T(8,128)S(1)} collective-permute-done((f32[8,32,512]{2,1,0:T(8,128)S(1)}, f32[8,32,512]{2,1,0:T(8,128)S(1)}, u32[]{:S(2)}, u32[]{:S(2)}) %collective-permute-start.1) | collective-permute-done | bytes 524320 | tf_op jit(solution)/shard_map/while/body/eval_jaxpr/ppermute | solution.py:10
  349.3 7.5 %collective-permute-done = f32[8,32,512]{2,1,0:T(8,128)S(1)} collective-permute-done((f32[8,32,512]{2,1,0:T(8,128)S(1)}, f32[8,32,512]{2,1,0:T(8,128)S(1)}, u32[]{:S(2)}, u32[]{:S(2)}) %collective-permute-start) | collective-permute-done | bytes 524320 | tf_op jit(solution)/shard_map/while/body/eval_jaxpr/ppermute | solution.py:10
  356.8 5.6 %collective-permute-done.1 = f32[8,32,512]{2,1,0:T(8,128)S(1)} collective-permute-done((f32[8,32,512]{2,1,0:T(8,128)S(1)}, f32[8,32,512]{2,1,0:T(8,128)S(1)}, u32[]{:S(2)}, u32[]{:S(2)}) %collective-permute-start.1) | collective-permute-done | bytes 524320 | tf_op jit(solution)/shard_map/while/body/eval_jaxpr/ppermute | solution.py:10
  365.5 4.4 %collective-permute-start.4 = (bf16[4,1,32,2,512]{4,2,3,1,0:T(8,128)(2,1)S(1)}, bf16[4,1,32,2,512]{4,2,3,1,0:T(8,128)(2,1)S(1)}, u32[]{:S(2)}, u32[]{:S(2)}) collective-permute-start(bf16[4,1,32,2,512]{4,2,3,1,0:T(8,128)(2,1)S(1)} %get-tuple-element.141), channel_id=1, source_target_pairs={{0,1},{1,2},{2,3},{4,5},{5,6},{6,7},{8,9},{9,10},{10,11},{12,13},{... | collective-permute-start | bytes 786440 | tf_op jit(solution)/shard_map/ppermute | solution.py:21
  374.9 3.9 fusion.5
  389.6 8.6 %fusion.19 = bf16[4,8,32,512]{3,2,1,0:T(8,128)(2,1)} fusion(bf16[4,8,32,512]{3,2,1,0:T(8,128)(2,1)S(1)} %copy-done.2, f32[4,8,32,512,1]{3,2,4,1,0:T(8,128)} %fusion.11, f32[4,8,32,512,1]{3,2,4,1,0:T(8,128)S(1)} %fusion.22, f32[4,8,32,512,1]{3,2,4,1,0:T(8,128)S(1)} %fusion.24, f32[4,8,32,512,1]{3,2,4,1,0:T(8,128)S(1)} %fusion.32, ...), kind=kOutput, calls=%fused_computation.33 | convolution fusion | flops 1113587712 | bytes 22022144 | tf_op jit(solution)/shard_map/dot_general | solution.py:59
  (89 shorter events, 100.8 us)
Async XLA Ops:
  6.5 8.4 %copy-start.5 = (f32[512]{0:T(512)S(1)}, f32[512]{0:T(512)}, u32[]{:S(2)}) copy-start(f32[512]{0:T(512)} %param.15) | copy-start | bytes 6148
  6.5 8.4 %copy-start.4 = (f32[8,32,2,512]{3,2,1,0:T(2,128)S(1)}, f32[8,32,2,512]{3,2,1,0:T(2,128)}, u32[]{:S(2)}) copy-start(f32[8,32,2,512]{3,2,1,0:T(2,128)} %param.16) | copy-start | bytes 3145732
  6.5 167.5 %all-gather.3.cloned.1.call-start = ((), (), s32[]{:S(2)}) async-start(), calls=%async_computation | async-start | bytes 11796480 | tf_op jit(solution)/shard_map/all_gather | solution.py:114
  7.3 365.0 %all-gather.5.cloned.1.call-start = ((), (), s32[]{:S(2)}) async-start(), calls=%async_computation.1 | async-start | bytes 11796480 | tf_op jit(solution)/shard_map/all_gather | solution.py:120
  9.0 7.3 %collective-permute-start.2 = (bf16[4,1,32,512]{3,2,1,0:T(8,128)(2,1)S(1)}, bf16[4,1,32,512]{3,2,1,0:T(8,128)(2,1)S(1)}, u32[]{:S(2)}, u32[]{:S(2)}) collective-permute-start(bf16[4,1,32,512]{3,2,1,0:T(8,128)(2,1)S(1)} %get-tuple-element.145), channel_id=1, source_target_pairs={{0,1},{1,2},{2,3},{4,5},{5,6},{6,7},{8,9},{9,10},{10,11},{12,13},{... | collective-permute-start | bytes 393224 | tf_op jit(solution)/shard_map/ppermute | solution.py:21
  12.5 6.9 %collective-permute-start.3 = (bf16[4,1,32,512]{3,2,1,0:T(8,128)(2,1)S(1)}, bf16[4,1,32,512]{3,2,1,0:T(8,128)(2,1)S(1)}, u32[]{:S(2)}, u32[]{:S(2)}) collective-permute-start(bf16[4,1,32,512]{3,2,1,0:T(8,128)(2,1)S(1)} %get-tuple-element.146), channel_id=1, source_target_pairs={{1,0},{2,1},{3,2},{5,4},{6,5},{7,6},{9,8},{10,9},{11,10},{13,12},{... | collective-permute-start | bytes 393224 | tf_op jit(solution)/shard_map/ppermute | solution.py:23
  241.8 11.4 %collective-permute-start = (f32[8,32,512]{2,1,0:T(8,128)S(1)}, f32[8,32,512]{2,1,0:T(8,128)S(1)}, u32[]{:S(2)}, u32[]{:S(2)}) collective-permute-start(f32[8,32,512]{2,1,0:T(8,128)S(1)} %get-tuple-element.268), channel_id=1, source_target_pairs={{0,4},{4,8},{8,12},{12,16},{16,20},{20,24},{24,28},{1,5},{5,9},{9,... | collective-permute-start | bytes 1572872 | tf_op jit(solution)/shard_map/while/body/eval_jaxpr/ppermute | solution.py:10
  243.7 15.1 %collective-permute-start.1 = (f32[8,32,512]{2,1,0:T(8,128)S(1)}, f32[8,32,512]{2,1,0:T(8,128)S(1)}, u32[]{:S(2)}, u32[]{:S(2)}) collective-permute-start(f32[8,32,512]{2,1,0:T(8,128)S(1)} %get-tuple-element.269), channel_id=1, source_target_pairs={{0,4},{4,8},{8,12},{12,16},{16,20},{20,24},{24,28},{1,5},{5,9},{9,... | collective-permute-start | bytes 1572872 | tf_op jit(solution)/shard_map/while/body/eval_jaxpr/ppermute | solution.py:10
  259.0 11.4 %collective-permute-start = (f32[8,32,512]{2,1,0:T(8,128)S(1)}, f32[8,32,512]{2,1,0:T(8,128)S(1)}, u32[]{:S(2)}, u32[]{:S(2)}) collective-permute-start(f32[8,32,512]{2,1,0:T(8,128)S(1)} %get-tuple-element.268), channel_id=1, source_target_pairs={{0,4},{4,8},{8,12},{12,16},{16,20},{20,24},{24,28},{1,5},{5,9},{9,... | collective-permute-start | bytes 1572872 | tf_op jit(solution)/shard_map/while/body/eval_jaxpr/ppermute | solution.py:10
  261.0 15.1 %collective-permute-start.1 = (f32[8,32,512]{2,1,0:T(8,128)S(1)}, f32[8,32,512]{2,1,0:T(8,128)S(1)}, u32[]{:S(2)}, u32[]{:S(2)}) collective-permute-start(f32[8,32,512]{2,1,0:T(8,128)S(1)} %get-tuple-element.269), channel_id=1, source_target_pairs={{0,4},{4,8},{8,12},{12,16},{16,20},{20,24},{24,28},{1,5},{5,9},{9,... | collective-permute-start | bytes 1572872 | tf_op jit(solution)/shard_map/while/body/eval_jaxpr/ppermute | solution.py:10
  276.3 11.4 %collective-permute-start = (f32[8,32,512]{2,1,0:T(8,128)S(1)}, f32[8,32,512]{2,1,0:T(8,128)S(1)}, u32[]{:S(2)}, u32[]{:S(2)}) collective-permute-start(f32[8,32,512]{2,1,0:T(8,128)S(1)} %get-tuple-element.268), channel_id=1, source_target_pairs={{0,4},{4,8},{8,12},{12,16},{16,20},{20,24},{24,28},{1,5},{5,9},{9,... | collective-permute-start | bytes 1572872 | tf_op jit(solution)/shard_map/while/body/eval_jaxpr/ppermute | solution.py:10
  278.2 15.1 %collective-permute-start.1 = (f32[8,32,512]{2,1,0:T(8,128)S(1)}, f32[8,32,512]{2,1,0:T(8,128)S(1)}, u32[]{:S(2)}, u32[]{:S(2)}) collective-permute-start(f32[8,32,512]{2,1,0:T(8,128)S(1)} %get-tuple-element.269), channel_id=1, source_target_pairs={{0,4},{4,8},{8,12},{12,16},{16,20},{20,24},{24,28},{1,5},{5,9},{9,... | collective-permute-start | bytes 1572872 | tf_op jit(solution)/shard_map/while/body/eval_jaxpr/ppermute | solution.py:10
  293.6 11.4 %collective-permute-start = (f32[8,32,512]{2,1,0:T(8,128)S(1)}, f32[8,32,512]{2,1,0:T(8,128)S(1)}, u32[]{:S(2)}, u32[]{:S(2)}) collective-permute-start(f32[8,32,512]{2,1,0:T(8,128)S(1)} %get-tuple-element.268), channel_id=1, source_target_pairs={{0,4},{4,8},{8,12},{12,16},{16,20},{20,24},{24,28},{1,5},{5,9},{9,... | collective-permute-start | bytes 1572872 | tf_op jit(solution)/shard_map/while/body/eval_jaxpr/ppermute | solution.py:10
  295.5 15.1 %collective-permute-start.1 = (f32[8,32,512]{2,1,0:T(8,128)S(1)}, f32[8,32,512]{2,1,0:T(8,128)S(1)}, u32[]{:S(2)}, u32[]{:S(2)}) collective-permute-start(f32[8,32,512]{2,1,0:T(8,128)S(1)} %get-tuple-element.269), channel_id=1, source_target_pairs={{0,4},{4,8},{8,12},{12,16},{16,20},{20,24},{24,28},{1,5},{5,9},{9,... | collective-permute-start | bytes 1572872 | tf_op jit(solution)/shard_map/while/body/eval_jaxpr/ppermute | solution.py:10
  310.9 11.4 %collective-permute-start = (f32[8,32,512]{2,1,0:T(8,128)S(1)}, f32[8,32,512]{2,1,0:T(8,128)S(1)}, u32[]{:S(2)}, u32[]{:S(2)}) collective-permute-start(f32[8,32,512]{2,1,0:T(8,128)S(1)} %get-tuple-element.268), channel_id=1, source_target_pairs={{0,4},{4,8},{8,12},{12,16},{16,20},{20,24},{24,28},{1,5},{5,9},{9,... | collective-permute-start | bytes 1572872 | tf_op jit(solution)/shard_map/while/body/eval_jaxpr/ppermute | solution.py:10
  312.8 15.1 %collective-permute-start.1 = (f32[8,32,512]{2,1,0:T(8,128)S(1)}, f32[8,32,512]{2,1,0:T(8,128)S(1)}, u32[]{:S(2)}, u32[]{:S(2)}) collective-permute-start(f32[8,32,512]{2,1,0:T(8,128)S(1)} %get-tuple-element.269), channel_id=1, source_target_pairs={{0,4},{4,8},{8,12},{12,16},{16,20},{20,24},{24,28},{1,5},{5,9},{9,... | collective-permute-start | bytes 1572872 | tf_op jit(solution)/shard_map/while/body/eval_jaxpr/ppermute | solution.py:10
  328.1 11.4 %collective-permute-start = (f32[8,32,512]{2,1,0:T(8,128)S(1)}, f32[8,32,512]{2,1,0:T(8,128)S(1)}, u32[]{:S(2)}, u32[]{:S(2)}) collective-permute-start(f32[8,32,512]{2,1,0:T(8,128)S(1)} %get-tuple-element.268), channel_id=1, source_target_pairs={{0,4},{4,8},{8,12},{12,16},{16,20},{20,24},{24,28},{1,5},{5,9},{9,... | collective-permute-start | bytes 1572872 | tf_op jit(solution)/shard_map/while/body/eval_jaxpr/ppermute | solution.py:10
  330.1 15.1 %collective-permute-start.1 = (f32[8,32,512]{2,1,0:T(8,128)S(1)}, f32[8,32,512]{2,1,0:T(8,128)S(1)}, u32[]{:S(2)}, u32[]{:S(2)}) collective-permute-start(f32[8,32,512]{2,1,0:T(8,128)S(1)} %get-tuple-element.269), channel_id=1, source_target_pairs={{0,4},{4,8},{8,12},{12,16},{16,20},{20,24},{24,28},{1,5},{5,9},{9,... | collective-permute-start | bytes 1572872 | tf_op jit(solution)/shard_map/while/body/eval_jaxpr/ppermute | solution.py:10
  345.4 11.4 %collective-permute-start = (f32[8,32,512]{2,1,0:T(8,128)S(1)}, f32[8,32,512]{2,1,0:T(8,128)S(1)}, u32[]{:S(2)}, u32[]{:S(2)}) collective-permute-start(f32[8,32,512]{2,1,0:T(8,128)S(1)} %get-tuple-element.268), channel_id=1, source_target_pairs={{0,4},{4,8},{8,12},{12,16},{16,20},{20,24},{24,28},{1,5},{5,9},{9,... | collective-permute-start | bytes 1572872 | tf_op jit(solution)/shard_map/while/body/eval_jaxpr/ppermute | solution.py:10
  347.3 15.1 %collective-permute-start.1 = (f32[8,32,512]{2,1,0:T(8,128)S(1)}, f32[8,32,512]{2,1,0:T(8,128)S(1)}, u32[]{:S(2)}, u32[]{:S(2)}) collective-permute-start(f32[8,32,512]{2,1,0:T(8,128)S(1)} %get-tuple-element.269), channel_id=1, source_target_pairs={{0,4},{4,8},{8,12},{12,16},{16,20},{20,24},{24,28},{1,5},{5,9},{9,... | collective-permute-start | bytes 1572872 | tf_op jit(solution)/shard_map/while/body/eval_jaxpr/ppermute | solution.py:10
  365.5 9.4 %collective-permute-start.4 = (bf16[4,1,32,2,512]{4,2,3,1,0:T(8,128)(2,1)S(1)}, bf16[4,1,32,2,512]{4,2,3,1,0:T(8,128)(2,1)S(1)}, u32[]{:S(2)}, u32[]{:S(2)}) collective-permute-start(bf16[4,1,32,2,512]{4,2,3,1,0:T(8,128)(2,1)S(1)} %get-tuple-element.141), channel_id=1, source_target_pairs={{0,1},{1,2},{2,3},{4,5},{5,6},{6,7},{8,9},{9,10},{10,11},{12,13},{... | collective-permute-start | bytes 786440 | tf_op jit(solution)/shard_map/ppermute | solution.py:21
  369.9 9.0 %collective-permute-start.5 = (bf16[4,1,32,2,512]{4,2,3,1,0:T(8,128)(2,1)S(1)}, bf16[4,1,32,2,512]{4,2,3,1,0:T(8,128)(2,1)S(1)}, u32[]{:S(2)}, u32[]{:S(2)}) collective-permute-start(bf16[4,1,32,2,512]{4,2,3,1,0:T(8,128)(2,1)S(1)} %get-tuple-element.142), channel_id=1, source_target_pairs={{1,0},{2,1},{3,2},{5,4},{6,5},{7,6},{9,8},{10,9},{11,10},{13,12},{... | collective-permute-start | bytes 786440 | tf_op jit(solution)/shard_map/ppermute | solution.py:23
  372.3 8.4 %slice-start = ((s8[9437184]{0:T(1024)(128)(4,1)}), s8[4194304]{0:T(1024)(128)(4,1)S(1)}, s32[]{:S(2)}) async-start(s8[9437184]{0:T(1024)(128)(4,1)} %bitcast.210), calls=%async_computation.2 | async-start | bytes 8388608
  372.3 8.4 %slice-start.1 = ((s8[9437184]{0:T(1024)(128)(4,1)}), s8[4194304]{0:T(1024)(128)(4,1)S(1)}, s32[]{:S(2)}) async-start(s8[9437184]{0:T(1024)(128)(4,1)} %bitcast.210), calls=%async_computation.3 | async-start | bytes 8388608
  (7 other events, 32.9 us)
Sparse Core Ops, SparseCore 0:
  8.9 165.1 all-gather.2
  175.6 164.9 all-gather.4
where the time goes:
time: 406 us; the launch traced here: 405 us
  waiting for transfers between devices  248 us (61%)
  matrix products  61.8 us (15%)
  starting transfers between devices  41.7 us (10%)
  local copies, waits for them, and re-layouts  21.8 us (5%)
  other arithmetic  17.6 us (4%)
  between operations  13.7 us (3%)
    all_gather x1, waiting for transfers between devices, on_device(): lax.all_gather(weight_in, 'rows', axis=1, tiled=True)  154 us
    ppermute x14, waiting for transfers between devices, passed_along(): lax.ppermute(value, axis, [(source, source + steps) for source in range(f...  89.9 us
    dot_general x9, matrix products, in_term(): lax.dot_general(window, weight_tap, (((3,), (1,)), ((), ())), preferred_e...  37.8 us
    ppermute x14, starting transfers between devices, passed_along(): lax.ppermute(value, axis, [(source, source + steps) for source in range(f...  29.1 us
    dot_general x9, matrix products, out_term(): lax.dot_general(window, piece[tap_index], (((3, 4), (0, 1)), ((), ())), p...  24 us
    dynamic_update_slice x4, other arithmetic, run_states(): lax.scan(advance, (begin_re, begin_im), (driven[..., 0, :], driven[..., 1...  9.82 us
  transfers between devices with their start and end apart: 20, of which 16 were waited for; matrix products, arithmetic and copies ran while one was open for 20% of the time, Pallas kernels for 0%

commit v1 on v0

--- a/solution.py
+++ b/solution.py
@@ -84,19 +84,18 @@
     (tail_re, tail_im), (local_re, local_im) = lax.scan(
         advance, (begin_re, begin_im), (driven[..., 0, :], driven[..., 1, :])
     )
-    span_mod = jnp.exp(-log_rate * frame_count)
-    span_re = span_mod * jnp.cos(angle * frame_count)
-    span_im = span_mod * jnp.sin(angle * frame_count)
-
-    def relay(turn_index, carried):
-        prior_re, prior_im = carried
-        sent_re = span_re * prior_re - span_im * prior_im + tail_re
-        sent_im = span_re * prior_im + span_im * prior_re + tail_im
-        return passed_along((sent_re, sent_im), "tm", 1)
-
-    carry_re, carry_im = lax.fori_loop(
-        0, lax.axis_size("tm") - 1, relay, (jnp.zeros_like(tail_re), jnp.zeros_like(tail_im))
-    )
+    carry_re, carry_im = passed_along((tail_re, tail_im), "tm", 1)
+    reach = 1
+    while reach < lax.axis_size("tm"):
+        far_re, far_im = passed_along((carry_re, carry_im), "tm", reach)
+        jump_mod = jnp.exp(-log_rate * (frame_count * reach))
+        jump_re = jump_mod * jnp.cos(angle * (frame_count * reach))
+        jump_im = jump_mod * jnp.sin(angle * (frame_count * reach))
+        carry_re, carry_im = (
+            carry_re + jump_re * far_re - jump_im * far_im,
+            carry_im + jump_re * far_im + jump_im * far_re,
+        )
+        reach *= 2
     step_count = jnp.arange(1, frame_count + 1, dtype=jnp.float32)[:, None, None, None]
     power_mod = jnp.exp(-log_rate * step_count)
     power_re = power_mod * jnp.cos(angle * step_count)
@@ -106,18 +105,25 @@
     return jnp.stack([states_re, states_im], 3).astype(jnp.bfloat16)
 
 
+def gathered(piece, axis):
+    count = lax.axis_size("tm")
+    width = piece.shape[axis] // count
+    own = lax.dynamic_slice_in_dim(piece, lax.axis_index("tm") * width, width, axis)
+    return lax.all_gather(own, ("rows", "tm"), axis=axis, tiled=True)
+
+
 def on_device(frames_in, weight_in, weight_out, log_decay, rotation, start_state, skip_gain):
     frame_count, band_rows, columns, channels = frames_in.shape
     extended = extended_2(frames_in, (("rows", 1),), 1)
     padded = pad_field(extended, 0)
     driven = in_term(
-        padded, lax.all_gather(weight_in, "rows", axis=1, tiled=True), band_rows, columns
+        padded, gathered(weight_in, 1), band_rows, columns
     )
     held = run_states(driven, start_state[:, :, 0, :], start_state[:, :, 1, :], log_decay, rotation)
     held = extended_2(held, (("rows", 1),), 1)
     held_padded = pad_field(held, 0)
     mixing = out_term(
-        held_padded, lax.all_gather(weight_out, "rows", axis=2, tiled=True), band_rows, columns
+        held_padded, gathered(weight_out, 2), band_rows, columns
     )
     pre_act = mixing + skip_gain * frames_in.astype(jnp.float32)
     return jax.nn.gelu(pre_act, approximate=False).astype(jnp.bfloat16)

time: 406 us -> 282 us (0.69)
  waiting for transfers between devices: 248 us -> 132 us
  starting transfers between devices: 41.7 us -> 27.6 us
  local copies, waits for them, and re-layouts: 21.8 us -> 28.1 us
    all_gather x2, waiting for transfers between devices: 154 us -> 69.9 us  [gathered(): return lax.all_gather(own, ('rows', 'tm'), axis=axis, tiled=True)]
    ppermute x14 -> x8, waiting for transfers between devices: 89.9 us -> 61.7 us  [passed_along(): lax.ppermute(value, axis, [(source, source + steps) for source in range(f...]
    ppermute x14 -> x8, starting transfers between devices: 29.1 us -> 15 us  [passed_along(): lax.ppermute(value, axis, [(source, source + steps) for source in range(f...]
  transfers between devices with their start and end apart: 20 -> 14, of which waited for: 16 -> 10; matrix products, arithmetic and copies ran while one was open for 20% -> 30% of each run, Pallas kernels for 0% -> 0%
where the time goes in v1:
time: 282 us; the launch traced here: 281 us
  waiting for transfers between devices  132 us (47%)
  matrix products  61.8 us (22%)
  local copies, waits for them, and re-layouts  28.1 us (10%)
  starting transfers between devices  27.6 us (10%)
  other arithmetic  17.7 us (6%)
  between operations  13.7 us (5%)
    all_gather x2, waiting for transfers between devices, gathered(): return lax.all_gather(own, ('rows', 'tm'), axis=axis, tiled=True)  69.9 us
    ppermute x8, waiting for transfers between devices, passed_along(): lax.ppermute(value, axis, [(source, source + steps) for source in range(f...  61.7 us
    dot_general x9, matrix products, in_term(): lax.dot_general(window, weight_tap, (((3,), (1,)), ((), ())), preferred_e...  37.6 us
    dot_general x9, matrix products, out_term(): lax.dot_general(window, piece[tap_index], (((3, 4), (0, 1)), ((), ())), p...  24.2 us
    ppermute x8, starting transfers between devices, passed_along(): lax.ppermute(value, axis, [(source, source + steps) for source in range(f...  15 us
    dynamic_update_slice x4, other arithmetic, run_states(): lax.scan(advance, (begin_re, begin_im), (driven[..., 0, :], driven[..., 1...  10.5 us
    slice x1, local copies, waits for them, and re-layouts, run_states(): driven[..., 1, :]  7.86 us
    reshape x1, local copies, waits for them, and re-layouts, in_term(): return summed.reshape(padded.shape[0], height, columns, parts, state_width)  6.57 us
  transfers between devices with their start and end apart: 14, of which 10 were waited for; matrix products, arithmetic and copies ran while one was open for 30% of the time, Pallas kernels for 0%

profile of v1, /device:TPU:12, one launch (start us, length us, event | category | flops | bytes accessed | tf_op | source)
XLA Modules:
  0.0 281.3 jit_solution(2158612243905289292)
XLA Ops:
  11.8 3.5 %collective-permute-start = (bf16[4,1,32,512]{3,2,1,0:T(8,128)(2,1)S(1)}, bf16[4,1,32,512]{3,2,1,0:T(8,128)(2,1)S(1)}, u32[]{:S(2)}, u32[]{:S(2)}) collective-permute-start(bf16[4,1,32,512]{3,2,1,0:T(8,128)(2,1)S(1)} %get-tuple-element.95), channel_id=1, source_target_pairs={{0,1},{1,2},{2,3},{4,5},{5,6},{6,7},{8,9},{9,10},{10,11},{12,13},{... | collective-permute-start | bytes 393224 | tf_op jit(solution)/shard_map/ppermute | solution.py:21
  23.0 69.9 %all-gather.3.cloned.1.call-done = bf16[2,512,4608]{2,1,0:T(8,128)(2,1)} async-done(((bf16[2,16,4608]{2,1,0:T(8,128)(2,1)}), bf16[2,512,4608]{2,1,0:T(8,128)(2,1)}) %all-gather.3.cloned.1.call-update) | async-done | bytes 9437200 | tf_op jit(solution)/shard_map/all_gather | solution.py:112
  95.5 4.9 %fusion.59 = f32[4,8,32,1024]{3,2,1,0:T(8,128)} fusion(bf16[4,1,32,512]{3,2,1,0:T(8,128)(2,1)S(1)} %collective-permute-done.1, bf16[4,8,32,512]{3,2,1,0:T(8,128)(2,1)S(1)} %copy-done.2, bf16[1024,4608]{1,0:T(8,128)(2,1)} %bitcast.212), kind=kOutput, calls=%fused_computation.89 | convolution fusion | flops 1076101120 | bytes 6422528 | tf_op jit(solution)/shard_map/dot_general | solution.py:47
  100.4 3.3 %fusion.67 = f32[4,8,32,1024]{3,2,1,0:T(8,128)} fusion(bf16[1024,4608]{1,0:T(8,128)(2,1)S(1)} %bitcast.214, bf16[4,10,34,512]{3,2,1,0:T(8,128)(2,1)S(1)} %fusion.52), kind=kOutput, calls=%fused_computation.109 | convolution fusion | flops 1073741824 | bytes 6291456 | tf_op jit(solution)/shard_map/dot_general | solution.py:47
  103.7 3.3 %fusion.69 = f32[4,8,32,1024]{3,2,1,0:T(8,128)} fusion(bf16[1024,4608]{1,0:T(8,128)(2,1)S(1)} %bitcast.215, bf16[4,10,34,512]{3,2,1,0:T(8,128)(2,1)S(1)} %fusion.52), kind=kOutput, calls=%fused_computation.112 | convolution fusion | flops 1073741824 | bytes 6291456 | tf_op jit(solution)/shard_map/dot_general | solution.py:47
  107.0 3.3 %fusion.72 = f32[4,8,32,1024]{3,2,1,0:T(8,128)} fusion(bf16[1024,4608]{1,0:T(8,128)(2,1)S(1)} %bitcast.216, bf16[4,10,34,512]{3,2,1,0:T(8,128)(2,1)S(1)} %fusion.52), kind=kOutput, calls=%fused_computation.117 | convolution fusion | flops 1073741824 | bytes 6291456 | tf_op jit(solution)/shard_map/dot_general | solution.py:47
  110.4 3.3 %fusion.74 = f32[4,8,32,1024]{3,2,1,0:T(8,128)} fusion(bf16[1024,4608]{1,0:T(8,128)(2,1)S(1)} %bitcast.217, bf16[4,10,34,512]{3,2,1,0:T(8,128)(2,1)S(1)} %fusion.52), kind=kOutput, calls=%fused_computation.120 | convolution fusion | flops 1073741824 | bytes 6291456 | tf_op jit(solution)/shard_map/dot_general | solution.py:47
  113.7 3.3 %fusion.76 = f32[4,8,32,1024]{3,2,1,0:T(8,128)} fusion(bf16[1024,4608]{1,0:T(8,128)(2,1)S(1)} %bitcast.218, bf16[4,10,34,512]{3,2,1,0:T(8,128)(2,1)S(1)} %fusion.52), kind=kOutput, calls=%fused_computation.124 | convolution fusion | flops 1073741824 | bytes 6291456 | tf_op jit(solution)/shard_map/dot_general | solution.py:47
  118.2 12.3 %fusion.4 = f32[4,8,32,1024]{3,2,1,0:T(8,128)} fusion(f32[4,8,32,1024]{3,2,1,0:T(8,128)} %fusion.59, f32[4,8,32,1024]{3,2,1,0:T(8,128)} %fusion.67, f32[4,8,32,1024]{3,2,1,0:T(8,128)} %fusion.69, f32[1024,4,8,32]{0,3,2,1:T(8,128)S(1)} %fusion.71, f32[4,8,32,1024]{3,2,1,0:T(8,128)} %fusion.72, f32[4,8,32,1024]{3,2,1,0:T(8,128)} %fusion.74, ...), kind=kOutput, calls=%fused_computation.13 | convolution fusion | flops 1082130432 | bytes 39845888 | tf_op jit(solution)/shard_map/dot_general | solution.py:47
  130.5 6.6 %reshape.136 = f32[4,8,32,2,512]{4,3,2,1,0:T(2,128)} reshape(f32[4,8,32,1024]{3,2,1,0:T(8,128)} %fusion.4) | data formatting | bytes 8388608 | tf_op jit(solution)/shard_map/reshape | solution.py:50
  137.1 7.9 %fusion.87 = (f32[4,8,32,1,512]{4,3,2,1,0:T(1,128)S(1)}, f32[4,8,32,1,512]{4,3,2,1,0:T(1,128)S(1)}) fusion(f32[4,8,32,2,512]{4,3,2,1,0:T(2,128)} %reshape.136), kind=kLoop, calls=%fused_computation.162 | loop fusion | bytes 8388608 | tf_op jit(solution)/shard_map/slice | solution.py:85
  150.8 10.5 %while.16 = (s32[]{:T(128)}, f32[8,32,512]{2,1,0:T(8,128)S(1)}, f32[8,32,512]{2,1,0:T(8,128)S(1)}, f32[4,8,32,512]{3,2,1,0:T(8,128)}, f32[4,8,32,512]{3,2,1,0:T(...) while((s32[]{:T(128)}, f32[8,32,512]{2,1,0:T(8,128)S(1)}, ...), condition=%wide.region_1.2_spmd, body=%wide.region_0.1_spmd.sunk | while | flops 1048578 | bytes 4199013 | solution.py:84
  165.7 6.9 %collective-permute-done.2 = f32[8,32,512]{2,1,0:T(8,128)S(1)} collective-permute-done((f32[8,32,512]{2,1,0:T(8,128)S(1)}, f32[8,32,512]{2,1,0:T(8,128)S(1)}, u32[]{:S(2)}, u32[]{:S(2)}) %collective-permute-start.2) | collective-permute-done | bytes 524320 | tf_op jit(solution)/shard_map/ppermute | solution.py:10
  174.6 3.7 %collective-permute-done.4 = f32[8,32,512]{2,1,0:T(8,128)S(1)} collective-permute-done((f32[8,32,512]{2,1,0:T(8,128)S(1)}, f32[8,32,512]{2,1,0:T(8,128)S(1)}, u32[]{:S(2)}, u32[]{:S(2)}) %collective-permute-start.4) | collective-permute-done | bytes 524320 | tf_op jit(solution)/shard_map/ppermute | solution.py:10
  180.2 3.9 %collective-permute-done.3 = f32[8,32,512]{2,1,0:T(8,128)S(1)} collective-permute-done((f32[8,32,512]{2,1,0:T(8,128)S(1)}, f32[8,32,512]{2,1,0:T(8,128)S(1)}, u32[]{:S(2)}, u32[]{:S(2)}) %collective-permute-start.3) | collective-permute-done | bytes 524320 | tf_op jit(solution)/shard_map/ppermute | solution.py:10
  184.0 5.6 %collective-permute-done.5 = f32[8,32,512]{2,1,0:T(8,128)S(1)} collective-permute-done((f32[8,32,512]{2,1,0:T(8,128)S(1)}, f32[8,32,512]{2,1,0:T(8,128)S(1)}, u32[]{:S(2)}, u32[]{:S(2)}) %collective-permute-start.5) | collective-permute-done | bytes 524320 | tf_op jit(solution)/shard_map/ppermute | solution.py:10
  193.8 13.7 %collective-permute-done.6 = f32[8,32,512]{2,1,0:T(8,128)S(1)} collective-permute-done((f32[8,32,512]{2,1,0:T(8,128)S(1)}, f32[8,32,512]{2,1,0:T(8,128)S(1)}, u32[]{:S(2)}, u32[]{:S(2)}) %collective-permute-start.6) | collective-permute-done | bytes 524320 | tf_op jit(solution)/shard_map/ppermute | solution.py:10
  207.5 7.4 %collective-permute-done.7 = f32[8,32,512]{2,1,0:T(8,128)S(1)} collective-permute-done((f32[8,32,512]{2,1,0:T(8,128)S(1)}, f32[8,32,512]{2,1,0:T(8,128)S(1)}, u32[]{:S(2)}, u32[]{:S(2)}) %collective-permute-start.7) | collective-permute-done | bytes 524320 | tf_op jit(solution)/shard_map/ppermute | solution.py:10
  218.2 13.9 %collective-permute-done.8 = f32[8,32,512]{2,1,0:T(8,128)S(1)} collective-permute-done((f32[8,32,512]{2,1,0:T(8,128)S(1)}, f32[8,32,512]{2,1,0:T(8,128)S(1)}, u32[]{:S(2)}, u32[]{:S(2)}) %collective-permute-start.8) | collective-permute-done | bytes 524320 | tf_op jit(solution)/shard_map/ppermute | solution.py:10
  232.1 6.5 %collective-permute-done.9 = f32[8,32,512]{2,1,0:T(8,128)S(1)} collective-permute-done((f32[8,32,512]{2,1,0:T(8,128)S(1)}, f32[8,32,512]{2,1,0:T(8,128)S(1)}, u32[]{:S(2)}, u32[]{:S(2)}) %collective-permute-start.9) | collective-permute-done | bytes 524320 | tf_op jit(solution)/shard_map/ppermute | solution.py:10
  240.6 3.0 %collective-permute-start.10 = (bf16[4,1,32,2,512]{4,2,3,1,0:T(8,128)(2,1)}, bf16[4,1,32,2,512]{4,2,3,1,0:T(8,128)(2,1)}, u32[]{:S(2)}, u32[]{:S(2)}) collective-permute-start(bf16[4,1,32,2,512]{4,2,3,1,0:T(8,128)(2,1)} %get-tuple-element.85), channel_id=1, source_target_pairs={{0,1},{1,2},{2,3},{4,5},{5,6},{6,7},{8,9},{9,10},{10,11},{12,13},{... | collective-permute-start | bytes 786440 | tf_op jit(solution)/shard_map/ppermute | solution.py:21
  243.6 3.7 %collective-permute-start.11 = (bf16[4,1,32,2,512]{4,2,3,1,0:T(8,128)(2,1)}, bf16[4,1,32,2,512]{4,2,3,1,0:T(8,128)(2,1)S(1)}, u32[]{:S(2)}, u32[]{:S(2)}) collective-permute-start(bf16[4,1,32,2,512]{4,2,3,1,0:T(8,128)(2,1)} %get-tuple-element.86), channel_id=1, source_target_pairs={{1,0},{2,1},{3,2},{5,4},{6,5},{7,6},{9,8},{10,9},{11,10},{13,12},{... | collective-permute-start | bytes 786440 | tf_op jit(solution)/shard_map/ppermute | solution.py:23
  250.0 4.0 %fusion.9 = f32[4,8,32,512,1]{3,2,4,1,0:T(8,128)} fusion(bf16[4,8,32,1,512]{4,2,3,1,0:T(8,128)(2,1)S(1)} %get-tuple-element.88, bf16[4,8,32,1,512]{4,2,3,1,0:T(8,128)(2,1)S(1)} %get-tuple-element.87, bf16[4,1,32,2,512]{4,2,3,1,0:T(8,128)(2,1)} %collective-permute-done.10, bf16[9,2,512,512]{3,2,1,0:T(8,128)(2,1)} %all-gather.5.cloned.1.call-done), kind=kOutput, calls=%fused_computation.21 | convolution fusion | flops 1080819712 | bytes 5505024 | tf_op jit(solution)/shard_map/dot_general | solution.py:59
  265.7 8.7 %fusion.23 = bf16[4,8,32,512]{3,2,1,0:T(8,128)(2,1)} fusion(bf16[4,8,32,512]{3,2,1,0:T(8,128)(2,1)S(1)} %copy-done.2, f32[4,8,32,512,1]{3,2,4,1,0:T(8,128)} %fusion.15, f32[4,8,32,512,1]{3,2,4,1,0:T(8,128)S(1)} %fusion.26, f32[4,8,32,512,1]{3,2,4,1,0:T(8,128)S(1)} %fusion.28, f32[4,8,32,512,1]{3,2,4,1,0:T(8,128)S(1)} %fusion.36, ...), kind=kOutput, calls=%fused_computation.35 | convolution fusion | flops 1113587712 | bytes 22022144 | tf_op jit(solution)/shard_map/dot_general | solution.py:59
  (76 shorter events, 64.9 us)
Async XLA Ops:
  6.5 86.3 %all-gather.3.cloned.1.call-start = ((), (), s32[]{:S(2)}) async-start(), calls=%async_computation | async-start | bytes 9732096 | tf_op jit(solution)/shard_map/all_gather | solution.py:112
  9.0 238.4 %all-gather.5.cloned.1.call-start = ((), (), s32[]{:S(2)}) async-start(), calls=%async_computation.1 | async-start | bytes 9732096 | tf_op jit(solution)/shard_map/all_gather | solution.py:112
  11.8 9.6 %collective-permute-start = (bf16[4,1,32,512]{3,2,1,0:T(8,128)(2,1)S(1)}, bf16[4,1,32,512]{3,2,1,0:T(8,128)(2,1)S(1)}, u32[]{:S(2)}, u32[]{:S(2)}) collective-permute-start(bf16[4,1,32,512]{3,2,1,0:T(8,128)(2,1)S(1)} %get-tuple-element.95), channel_id=1, source_target_pairs={{0,1},{1,2},{2,3},{4,5},{5,6},{6,7},{8,9},{9,10},{10,11},{12,13},{... | collective-permute-start | bytes 393224 | tf_op jit(solution)/shard_map/ppermute | solution.py:21
  15.3 6.9 %collective-permute-start.1 = (bf16[4,1,32,512]{3,2,1,0:T(8,128)(2,1)S(1)}, bf16[4,1,32,512]{3,2,1,0:T(8,128)(2,1)S(1)}, u32[]{:S(2)}, u32[]{:S(2)}) collective-permute-start(bf16[4,1,32,512]{3,2,1,0:T(8,128)(2,1)S(1)} %get-tuple-element.96), channel_id=1, source_target_pairs={{1,0},{2,1},{3,2},{5,4},{6,5},{7,6},{9,8},{10,9},{11,10},{13,12},{... | collective-permute-start | bytes 393224 | tf_op jit(solution)/shard_map/ppermute | solution.py:23
  17.6 3.7 %copy-start.7 = (f32[512]{0:T(512)S(1)}, f32[512]{0:T(512)}, u32[]{:S(2)}) copy-start(f32[512]{0:T(512)} %param.13) | copy-start | bytes 6148
  17.7 3.6 %copy-start.8 = (f32[512]{0:T(512)S(1)}, f32[512]{0:T(512)}, u32[]{:S(2)}) copy-start(f32[512]{0:T(512)} %param.12) | copy-start | bytes 6148
  17.7 4.5 %copy-start.2 = (bf16[4,8,32,512]{3,2,1,0:T(8,128)(2,1)S(1)}, bf16[4,8,32,512]{3,2,1,0:T(8,128)(2,1)}, u32[]{:S(2)}) copy-start(bf16[4,8,32,512]{3,2,1,0:T(8,128)(2,1)} %param.9) | copy-start | bytes 3145732
  92.8 7.5 %copy-start.4 = (bf16[2,512,4608]{2,1,0:T(8,128)(2,1)S(1)}, bf16[2,512,4608]{2,1,0:T(8,128)(2,1)}, u32[]{:S(2)}) copy-start(bf16[2,512,4608]{2,1,0:T(8,128)(2,1)} %all-gather.3.cloned.1.call-done) | copy-start | bytes 28311556
  161.3 11.4 %collective-permute-start.2 = (f32[8,32,512]{2,1,0:T(8,128)S(1)}, f32[8,32,512]{2,1,0:T(8,128)S(1)}, u32[]{:S(2)}, u32[]{:S(2)}) collective-permute-start(f32[8,32,512]{2,1,0:T(8,128)S(1)} %get-tuple-element.56), channel_id=1, source_target_pairs={{0,4},{4,8},{8,12},{12,16},{16,20},{20,24},{24,28},{1,5},{5,9},{9,... | collective-permute-start | bytes 1572872 | tf_op jit(solution)/shard_map/ppermute | solution.py:10
  163.4 14.8 %collective-permute-start.4 = (f32[8,32,512]{2,1,0:T(8,128)S(1)}, f32[8,32,512]{2,1,0:T(8,128)S(1)}, u32[]{:S(2)}, u32[]{:S(2)}) collective-permute-start(f32[8,32,512]{2,1,0:T(8,128)S(1)} %get-tuple-element.57), channel_id=1, source_target_pairs={{0,4},{4,8},{8,12},{12,16},{16,20},{20,24},{24,28},{1,5},{5,9},{9,... | collective-permute-start | bytes 1572872 | tf_op jit(solution)/shard_map/ppermute | solution.py:10
  172.6 11.4 %collective-permute-start.3 = (f32[8,32,512]{2,1,0:T(8,128)S(1)}, f32[8,32,512]{2,1,0:T(8,128)S(1)}, u32[]{:S(2)}, u32[]{:S(2)}) collective-permute-start(f32[8,32,512]{2,1,0:T(8,128)S(1)} %collective-permute-done.2), channel_id=1, source_target_pairs={{0,4},{4,8},{8,12},{12,16},{16,20},{20,24},{24,28},{1,5},{5,9},{9,... | collective-permute-start | bytes 1572872 | tf_op jit(solution)/shard_map/ppermute | solution.py:10
  178.3 11.4 %collective-permute-start.5 = (f32[8,32,512]{2,1,0:T(8,128)S(1)}, f32[8,32,512]{2,1,0:T(8,128)S(1)}, u32[]{:S(2)}, u32[]{:S(2)}) collective-permute-start(f32[8,32,512]{2,1,0:T(8,128)S(1)} %collective-permute-done.4), channel_id=1, source_target_pairs={{0,4},{4,8},{8,12},{12,16},{16,20},{20,24},{24,28},{1,5},{5,9},{9,... | collective-permute-start | bytes 1572872 | tf_op jit(solution)/shard_map/ppermute | solution.py:10
  189.9 17.6 %collective-permute-start.6 = (f32[8,32,512]{2,1,0:T(8,128)S(1)}, f32[8,32,512]{2,1,0:T(8,128)S(1)}, u32[]{:S(2)}, u32[]{:S(2)}) collective-permute-start(f32[8,32,512]{2,1,0:T(8,128)S(1)} %get-tuple-element.93), channel_id=1, source_target_pairs={{0,8},{4,12},{8,16},{12,20},{16,24},{20,28},{1,9},{5,13},{9,17},{1... | collective-permute-start | bytes 1572872 | tf_op jit(solution)/shard_map/ppermute | solution.py:10
  191.8 23.0 %collective-permute-start.7 = (f32[8,32,512]{2,1,0:T(8,128)S(1)}, f32[8,32,512]{2,1,0:T(8,128)S(1)}, u32[]{:S(2)}, u32[]{:S(2)}) collective-permute-start(f32[8,32,512]{2,1,0:T(8,128)S(1)} %get-tuple-element.94), channel_id=1, source_target_pairs={{0,8},{4,12},{8,16},{12,20},{16,24},{20,28},{1,9},{5,13},{9,17},{1... | collective-permute-start | bytes 1572872 | tf_op jit(solution)/shard_map/ppermute | solution.py:10
  214.9 24.0 %copy-start.6 = (f32[4,8,32,512]{3,2,1,0:T(8,128)S(1)}, f32[4,8,32,512]{3,2,1,0:T(8,128)}, u32[]{:S(2)}) copy-start(f32[4,8,32,512]{3,2,1,0:T(8,128)} %get-tuple-element.58) | copy-start | bytes 6291460
  215.1 23.8 %copy-start.5 = (f32[4,8,32,512]{3,2,1,0:T(8,128)S(1)}, f32[4,8,32,512]{3,2,1,0:T(8,128)}, u32[]{:S(2)}) copy-start(f32[4,8,32,512]{3,2,1,0:T(8,128)} %get-tuple-element.55) | copy-start | bytes 6291460
  215.1 17.0 %collective-permute-start.8 = (f32[8,32,512]{2,1,0:T(8,128)S(1)}, f32[8,32,512]{2,1,0:T(8,128)S(1)}, u32[]{:S(2)}, u32[]{:S(2)}) collective-permute-start(f32[8,32,512]{2,1,0:T(8,128)S(1)} %get-tuple-element.92), channel_id=1, source_target_pairs={{0,16},{4,20},{8,24},{12,28},{1,17},{5,21},{9,25},{13,29},{2,18},{... | collective-permute-start | bytes 1572872 | tf_op jit(solution)/shard_map/ppermute | solution.py:10
  216.7 21.9 %collective-permute-start.9 = (f32[8,32,512]{2,1,0:T(8,128)S(1)}, f32[8,32,512]{2,1,0:T(8,128)S(1)}, u32[]{:S(2)}, u32[]{:S(2)}) collective-permute-start(f32[8,32,512]{2,1,0:T(8,128)S(1)} %get-tuple-element.91), channel_id=1, source_target_pairs={{0,16},{4,20},{8,24},{12,28},{1,17},{5,21},{9,25},{13,29},{2,18},{... | collective-permute-start | bytes 1572872 | tf_op jit(solution)/shard_map/ppermute | solution.py:10
  240.6 9.4 %collective-permute-start.10 = (bf16[4,1,32,2,512]{4,2,3,1,0:T(8,128)(2,1)}, bf16[4,1,32,2,512]{4,2,3,1,0:T(8,128)(2,1)}, u32[]{:S(2)}, u32[]{:S(2)}) collective-permute-start(bf16[4,1,32,2,512]{4,2,3,1,0:T(8,128)(2,1)} %get-tuple-element.85), channel_id=1, source_target_pairs={{0,1},{1,2},{2,3},{4,5},{5,6},{6,7},{8,9},{9,10},{10,11},{12,13},{... | collective-permute-start | bytes 786440 | tf_op jit(solution)/shard_map/ppermute | solution.py:21
  243.6 10.4 %collective-permute-start.11 = (bf16[4,1,32,2,512]{4,2,3,1,0:T(8,128)(2,1)}, bf16[4,1,32,2,512]{4,2,3,1,0:T(8,128)(2,1)S(1)}, u32[]{:S(2)}, u32[]{:S(2)}) collective-permute-start(bf16[4,1,32,2,512]{4,2,3,1,0:T(8,128)(2,1)} %get-tuple-element.86), channel_id=1, source_target_pairs={{1,0},{2,1},{3,2},{5,4},{6,5},{7,6},{9,8},{10,9},{11,10},{13,12},{... | collective-permute-start | bytes 786440 | tf_op jit(solution)/shard_map/ppermute | solution.py:23
  247.4 9.4 %slice-start = ((s8[9437184]{0:T(1024)(128)(4,1)}), s8[4194304]{0:T(1024)(128)(4,1)S(1)}, s32[]{:S(2)}) async-start(s8[9437184]{0:T(1024)(128)(4,1)} %bitcast.220), calls=%async_computation.2 | async-start | bytes 8388608
  247.4 9.4 %slice-start.1 = ((s8[9437184]{0:T(1024)(128)(4,1)}), s8[4194304]{0:T(1024)(128)(4,1)S(1)}, s32[]{:S(2)}) async-start(s8[9437184]{0:T(1024)(128)(4,1)} %bitcast.220), calls=%async_computation.3 | async-start | bytes 8388608
  250.0 6.8 %slice-start.2 = ((s8[9437184]{0:T(1024)(128)(4,1)}), s8[1048576]{0:T(1024)(128)(4,1)S(1)}, s32[]{:S(2)}) async-start(s8[9437184]{0:T(1024)(128)(4,1)} %bitcast.220), calls=%async_computation.4 | async-start | bytes 2097152
  265.7 8.7 %copy-start.1 = (bf16[2,128,4608]{2,1,0:T(8,128)(2,1)S(1)}, bf16[2,128,4608]{2,1,0:T(8,128)(2,1)}, u32[]{:S(2)}) copy-start(bf16[2,128,4608]{2,1,0:T(8,128)(2,1)} %param.10) | copy-start | bytes 7077892
  (3 other events, 7.5 us)
Sparse Core Ops, SparseCore 0:
  10.3 82.5 all-gather.2
  95.8 80.4 all-gather.4
